TPU v7x, 128 devices: a whole 4x4x4 slice. The times are simulated.
128 devices in a mesh: pair: 2 (over core), batch: 4 (over y), vocab: 16 (over x, z).
Axes of the slice: x: 4, y: 4, z: 4, core: 2. Of those that a mesh axis runs over, the one named last changes fastest.
Arguments:
- hidden: bfloat16 [2, 512, 8192], P('pair', 'batch', 'vocab'), may hold values from -120 to 120
- norm_gain: bfloat16 [8192], P('vocab'), may hold values from 0.099609375 to 1.8984375
- head_weight: bfloat16 [8192, 65536], P(('pair', 'batch'), 'vocab'), may hold values from -1 to 1
Outputs:
- guided_logprobs: float32 [512, 65536], P(('pair', 'batch'), 'vocab')
- cond_logprobs: float32 [512, 65536], P(('pair', 'batch'), 'vocab')
All inputs are finite; a program needn't handle non-finite values.
Results may differ from a plain program's by a relative error of at most 0.007.
Values may be sent and summed in bfloat16 or wider, within the bound.
A program may use at most 128 MiB of HBM per device.

v0:
```python
import jax
import jax.numpy as jnp
from jax import lax
from jax.sharding import PartitionSpec as P

D = 8192
EPS = 1e-05
GUIDE = 1.5


def on_device(hidden, norm_gain, head_weight):
    rows = lax.all_gather(hidden[0], "vocab", axis=1, tiled=True)
    gain = lax.all_gather(norm_gain, "vocab", axis=0, tiled=True)
    wide = rows.astype(jnp.float32)
    total_sq = jnp.sum(wide * wide, axis=1)
    scaled = wide * lax.rsqrt(total_sq / D + EPS)[:, None] * gain.astype(jnp.float32)[None, :]
    features = scaled.astype(jnp.bfloat16)
    blocks = lax.all_to_all(features, ("pair", "batch"), split_axis=1, concat_axis=0, tiled=True)
    groups = lax.axis_size("pair") * lax.axis_size("batch")
    width = blocks.shape[1]
    out_rows = blocks.shape[0] // (2 * groups)
    ordered = blocks.reshape(2, groups, out_rows, width).transpose(1, 0, 2, 3).reshape(-1, width)
    logits = lax.psum_scatter(
        jnp.dot(ordered, head_weight, preferred_element_type=jnp.float32),
        ("pair", "batch"),
        scatter_dimension=0,
        tiled=True,
    )
    cond = logits[:out_rows]
    uncond = logits[out_rows:]
    guided = GUIDE * cond + (1.0 - GUIDE) * uncond
    peak_c = jnp.max(cond, axis=1)
    peak_g = jnp.max(guided, axis=1)
    local_c = jnp.sum(jnp.exp(cond - peak_c[:, None]), axis=1)
    local_g = jnp.sum(jnp.exp(guided - peak_g[:, None]), axis=1)
    stats = jnp.stack([peak_c, local_c, peak_g, local_g])
    every = lax.all_gather(stats, "vocab", axis=0)
    top_c = jnp.max(every[:, 0], axis=0)
    top_g = jnp.max(every[:, 2], axis=0)
    total_c = jnp.sum(every[:, 1] * jnp.exp(every[:, 0] - top_c[None, :]), axis=0)
    total_g = jnp.sum(every[:, 3] * jnp.exp(every[:, 2] - top_g[None, :]), axis=0)
    cond_out = cond - (top_c + jnp.log(total_c))[:, None]
    guided_out = guided - (top_g + jnp.log(total_g))[:, None]
    return (guided_out, cond_out)


def solution(mesh):
    in_specs = (P("pair", "batch", "vocab"), P("vocab"), P(("pair", "batch"), "vocab"))
    out_specs = (P(("pair", "batch"), "vocab"), P(("pair", "batch"), "vocab"))
    return jax.shard_map(
        on_device, mesh=mesh, in_specs=in_specs, out_specs=out_specs, check_vma=False
    )
```

profile of v0, /device:TPU:0, one launch (start us, length us, event | category | flops | bytes accessed | tf_op | source)
XLA Modules:
  0.0 317.6 jit_solution(5014193301131208361)
XLA Ops:
  7.2 0.0 all-gather.6.cloned.1.call-start
  7.2 1.7 copy.15
  8.9 0.0 all-gather.6.cloned.1.call-update
  8.9 0.0 reduce-scatter.2.cloned.1.call-start
  8.9 0.7 reshape.41
  9.6 24.7 %all-gather.2 = bf16[16,1,512]{2,1,0:T(2,128)(2,1)S(1)} all-gather(bf16[1,1,512]{2,1,0:T(2,128)(2,1)S(1)} %reshape.41), channel_id=1, replica_groups=mesh['pair'=2,'batch'=4,'vocab'=16] {'vocab'}, dimensions={0}, use_global_device_ids=true | all-gather | bytes 17408 | tf_op jit(solution)/shard_map/all_gather | solution.py:13
  34.4 24.1 %all-gather.6.cloned.1.call-done = bf16[1,128,8192]{1,2,0:T(8,128)(2,1)} async-done(((bf16[1,128,512]{1,2,0:T(8,128)(2,1)}), bf16[1,128,8192]{1,2,0:T(8,128)(2,1)}) %all-gather.6.cloned.1.call-update) | async-done | bytes 2097168 | tf_op jit(solution)/shard_map/all_gather | solution.py:12
  58.5 0.0 copy-start.1
  58.5 2.8 fusion
  61.3 0.0 copy-done.1
  61.3 3.5 %fusion.2 = bf16[128,8192]{0,1:T(8,128)(2,1)S(1)} fusion(bf16[1,128,8192]{1,2,0:T(8,128)(2,1)S(1)} %copy-done.1, f32[8192]{0:T(1024)S(1)} %bitcast.31, f32[128]{0:T(128)S(1)} %add_rsqrt_fusion), kind=kLoop, calls=%fused_computation.4 | loop fusion | flops 4194304 | bytes 4227584 | tf_op jit(solution)/shard_map/convert_element_type | solution.py:17
  64.8 30.7 %all_to_all.16 = bf16[128,8,1024]{0,2,1:T(8,128)(2,1)S(1)} all-to-all(bf16[128,8,1024]{0,2,1:T(8,128)(2,1)S(1)} %bitcast.27), channel_id=1, replica_groups=mesh['pair'=2,'batch'=4,'vocab'=16] {'pair','batch'}, dimensions={1} | all-to-all | bytes 4194304 | tf_op jit(solution)/shard_map/all_to_all | solution.py:18
  95.5 2.6 copy.16
  98.1 1.8 copy.17
  99.9 14.4 %fusion.6 = f32[1024,4096]{1,0:T(8,128)} fusion(bf16[1024,1024]{1,0:T(8,128)(2,1)S(1)} %bitcast.30, bf16[1024,4096]{1,0:T(8,128)(2,1)} %param.5), kind=kOutput, calls=%fused_computation.21 | convolution fusion | flops 8589934592 | bytes 27262976 | tf_op jit(solution)/shard_map/dot_general | solution.py:24
  114.3 0.0 reduce-scatter.2.cloned.1.call-update
  114.3 168.4 %reduce-scatter.2.cloned.1.call-done = f32[128,4096]{1,0:T(8,128)} async-done(((f32[1024,4096]{1,0:T(8,128)}), f32[128,4096]{1,0:T(8,128)}) %reduce-scatter.2.cloned.1.call-update) | async-done | bytes 2097168 | tf_op jit(solution)/shard_map/reduce_scatter | solution.py:23
  282.7 0.0 copy-start
  282.7 2.0 slice_reduce_fusion
  284.7 0.3 copy-done
  284.9 0.5 exponential_reduce_fusion.1
  285.5 23.5 %all-gather.3 = f32[16,4,64]{2,1,0:T(4,128)S(1)} all-gather(f32[1,4,64]{2,1,0:T(4,128)S(1)} %maximum_bitcast_fusion), channel_id=3, replica_groups=mesh['pair'=2,'batch'=4,'vocab'=16] {'vocab'}, dimensions={0}, use_global_device_ids=true | all-gather | bytes 17408 | tf_op jit(solution)/shard_map/all_gather | solution.py:37
  309.1 1.6 slice_subtract_fusion
  (8 shorter events, 0.2 us)
Async XLA Ops:
  7.2 51.3 %all-gather.6.cloned.1.call-start = ((), (), s32[]{:S(2)}) async-start(), calls=%async_computation.3 | async-start | bytes 2228224 | tf_op jit(solution)/shard_map/all_gather | solution.py:12
  8.9 273.8 %reduce-scatter.2.cloned.1.call-start = ((), (), s32[]{:S(2)}) async-start(), calls=%async_computation.2 | async-start | bytes 18874368 | tf_op jit(solution)/shard_map/reduce_scatter | solution.py:23
  58.5 2.8 copy-start.1
  282.7 2.2 copy-start
Sparse Core Ops, SparseCore 0:
  10.7 47.7 all-gather.5
  114.5 168.2 reduce-scatter.1
where the time goes:
time: 318 us
  waiting for transfers between devices  193 us (61%)
  blocking collectives  78.9 us (25%)
  matrix products  14.4 us (5%)
  between operations  14.1 us (4%)
  other arithmetic  10.6 us (3%)
  local copies, waits for them, and re-layouts  7.03 us (2%)
    reduce_scatter x1, waiting for transfers between devices, on_device(): lax.psum_scatter(jnp.dot(ordered, head_weight, preferred_element_type=jnp...  168 us
    all_to_all x1, blocking collectives, on_device(): lax.all_to_all(features, ('pair', 'batch'), split_axis=1, concat_axis=0,...  30.7 us
    all_gather x1, blocking collectives, on_device(): gain = lax.all_gather(norm_gain, 'vocab', axis=0, tiled=True)  24.7 us
    all_gather x1, waiting for transfers between devices, on_device(): rows = lax.all_gather(hidden[0], 'vocab', axis=1, tiled=True)  24.1 us
    all_gather x1, blocking collectives, on_device(): every = lax.all_gather(stats, 'vocab', axis=0)  23.5 us
    dot_general x1, matrix products, on_device(): jnp.dot(ordered, head_weight, preferred_element_type=jnp.float32)  14.4 us
  transfers between devices with their start and end apart: 2, of which 2 were waited for; matrix products, arithmetic and copies ran while one was open for 0% of the time, Pallas kernels for 0%

commit v1 on v0

--- a/solution.py
+++ b/solution.py
@@ -8,8 +8,27 @@
 GUIDE = 1.5
 
 
+def gather_around(x, axis, dim):
+    peers, here, rows = (lax.axis_size(axis), lax.axis_index(axis), x.shape[dim])
+    right = [(i, (i + 1) % peers) for i in range(peers)]
+    downward = [(i, (i - 1) % peers) for i in range(peers)]
+    out = jnp.zeros((*x.shape[:dim], peers * rows, *x.shape[dim + 1 :]), x.dtype)
+    out = lax.dynamic_update_slice_in_dim(out, x, here * rows, axis=dim)
+    from_left = from_right = x
+    half = peers // 2
+    for lap in range(1, half + 1):
+        from_left = lax.ppermute(from_left, axis, right)
+        out = lax.dynamic_update_slice_in_dim(out, from_left, (here - lap) % peers * rows, axis=dim)
+        if lap < peers - half:
+            from_right = lax.ppermute(from_right, axis, downward)
+            out = lax.dynamic_update_slice_in_dim(
+                out, from_right, (here + lap) % peers * rows, axis=dim
+            )
+    return out
+
+
 def on_device(hidden, norm_gain, head_weight):
-    rows = lax.all_gather(hidden[0], "vocab", axis=1, tiled=True)
+    rows = gather_around(hidden[0], "vocab", 1)
     gain = lax.all_gather(norm_gain, "vocab", axis=0, tiled=True)
     wide = rows.astype(jnp.float32)
     total_sq = jnp.sum(wide * wide, axis=1)

time: 318 us -> 351 us (1.10)
  starting transfers between devices: 0.08 us -> 40 us
    ppermute x0 -> x15, starting transfers between devices: none -> 40 us  [the longest x7 36.7 us: gather_around(): from_right = lax.ppermute(from_right, axis, downward)]
    ppermute x0 -> x15, waiting for transfers between devices: none -> 25.8 us  [the longest x8 25.8 us: gather_around(): from_left = lax.ppermute(from_left, axis, right)]
    all_gather x1 -> x0, waiting for transfers between devices: 24.1 us -> none  [on_device(): rows = lax.all_gather(hidden[0], 'vocab', axis=1, tiled=True)]
    all_gather x1, blocking collectives: 24.7 us -> 21.1 us  [on_device(): gain = lax.all_gather(norm_gain, 'vocab', axis=0, tiled=True)]
  transfers between devices with their start and end apart: 2 -> 16, of which waited for: 2 -> 8; matrix products, arithmetic and copies ran while one was open for 0% -> 0% of each run, Pallas kernels for 0% -> 0%
where the time goes in v1:
time: 351 us
  waiting for transfers between devices  191 us (54%)
  blocking collectives  75.4 us (21%)
  starting transfers between devices  40 us (11%)
  matrix products  14.4 us (4%)
  between operations  14.3 us (4%)
  other arithmetic  8.85 us (3%)
  local copies, waits for them, and re-layouts  6.99 us (2%)
    reduce_scatter x1, waiting for transfers between devices, on_device(): lax.psum_scatter(jnp.dot(ordered, head_weight, preferred_element_type=jnp...  165 us
    ppermute x7, starting transfers between devices, gather_around(): from_right = lax.ppermute(from_right, axis, downward)  36.7 us
    all_to_all x1, blocking collectives, on_device(): lax.all_to_all(features, ('pair', 'batch'), split_axis=1, concat_axis=0,...  30.8 us
    ppermute x8, waiting for transfers between devices, gather_around(): from_left = lax.ppermute(from_left, axis, right)  25.8 us
    all_gather x1, blocking collectives, on_device(): every = lax.all_gather(stats, 'vocab', axis=0)  23.5 us
    all_gather x1, blocking collectives, on_device(): gain = lax.all_gather(norm_gain, 'vocab', axis=0, tiled=True)  21.1 us
    dot_general x1, matrix products, on_device(): jnp.dot(ordered, head_weight, preferred_element_type=jnp.float32)  14.4 us
  transfers between devices with their start and end apart: 16, of which 8 were waited for; matrix products, arithmetic and copies ran while one was open for 0% of the time, Pallas kernels for 0%

profile of v1, /device:TPU:0, one launch (start us, length us, event | category | flops | bytes accessed | tf_op | source)
XLA Modules:
  0.0 351.2 jit_solution(10631374595467063336)
XLA Ops:
  7.2 0.0 reduce-scatter.2.cloned.1.call-start
  7.2 1.0 copy.15
  8.2 2.1 collective-permute-start
  10.3 4.4 %collective-permute-start.1 = (bf16[128,512]{0,1:T(8,128)(2,1)S(1)}, bf16[128,512]{0,1:T(8,128)(2,1)S(1)}, u32[]{:S(2)}, u32[]{:S(2)}) collective-permute-start(bf16[128,512]{0,1:T(8,128)(2,1)S(1)} %bitcast.30), channel_id=1, source_target_pairs={{0,15},{1,0},{2,1},{3,2},{4,3},{5,4},{6,5},{7,6},{8,7},{9,8},{10,9... | collective-permute-start | bytes 393224 | tf_op jit(solution)/shard_map/ppermute | solution.py:23
  14.7 0.7 reshape.39
  15.4 21.1 %all-gather.1 = bf16[16,1,512]{2,1,0:T(2,128)(2,1)S(1)} all-gather(bf16[1,1,512]{2,1,0:T(2,128)(2,1)S(1)} %reshape.39), channel_id=1, replica_groups=mesh['pair'=2,'batch'=4,'vocab'=16] {'vocab'}, dimensions={0}, use_global_device_ids=true | all-gather | bytes 17408 | tf_op jit(solution)/shard_map/all_gather | solution.py:32
  36.6 0.3 broadcast_in_dim.2
  36.9 0.0 collective-permute-done
  36.9 1.3 collective-permute-start.2
  38.2 0.0 collective-permute-done.1
  38.2 4.2 %collective-permute-start.3 = (bf16[128,512]{0,1:T(8,128)(2,1)S(1)}, bf16[128,512]{0,1:T(8,128)(2,1)S(1)}, u32[]{:S(2)}, u32[]{:S(2)}) collective-permute-start(bf16[128,512]{0,1:T(8,128)(2,1)S(1)} %collective-permute-done.1), channel_id=1, source_target_pairs={{0,15},{1,0},{2,1},{3,2},{4,3},{5,4},{6,5},{7,6},{8,7},{9,8},{10,9... | collective-permute-start | bytes 393224 | tf_op jit(solution)/shard_map/ppermute | solution.py:23
  42.4 4.0 %collective-permute-done.2 = bf16[128,512]{0,1:T(8,128)(2,1)S(1)} collective-permute-done((bf16[128,512]{0,1:T(8,128)(2,1)S(1)}, bf16[128,512]{0,1:T(8,128)(2,1)S(1)}, u32[]{:S(2)}, u32[]{:S(2)}) %collective-permute-start.2) | collective-permute-done | bytes 131104 | tf_op jit(solution)/shard_map/ppermute | solution.py:20
  46.4 0.0 collective-permute-start.4
  46.4 0.0 collective-permute-done.3
  46.4 5.6 %collective-permute-start.5 = (bf16[128,512]{0,1:T(8,128)(2,1)S(1)}, bf16[128,512]{0,1:T(8,128)(2,1)S(1)}, u32[]{:S(2)}, u32[]{:S(2)}) collective-permute-start(bf16[128,512]{0,1:T(8,128)(2,1)S(1)} %collective-permute-done.3), channel_id=1, source_target_pairs={{0,15},{1,0},{2,1},{3,2},{4,3},{5,4},{6,5},{7,6},{8,7},{9,8},{10,9... | collective-permute-start | bytes 393224 | tf_op jit(solution)/shard_map/ppermute | solution.py:23
  52.0 3.2 collective-permute-done.4
  55.2 0.0 collective-permute-start.6
  55.2 0.0 collective-permute-done.5
  55.2 5.6 %collective-permute-start.7 = (bf16[128,512]{0,1:T(8,128)(2,1)S(1)}, bf16[128,512]{0,1:T(8,128)(2,1)S(1)}, u32[]{:S(2)}, u32[]{:S(2)}) collective-permute-start(bf16[128,512]{0,1:T(8,128)(2,1)S(1)} %collective-permute-done.5), channel_id=1, source_target_pairs={{0,15},{1,0},{2,1},{3,2},{4,3},{5,4},{6,5},{7,6},{8,7},{9,8},{10,9... | collective-permute-start | bytes 393224 | tf_op jit(solution)/shard_map/ppermute | solution.py:23
  60.9 2.6 collective-permute-done.6
  63.5 0.0 collective-permute-start.8
  63.5 0.0 collective-permute-done.7
  63.5 5.6 %collective-permute-start.9 = (bf16[128,512]{0,1:T(8,128)(2,1)S(1)}, bf16[128,512]{0,1:T(8,128)(2,1)S(1)}, u32[]{:S(2)}, u32[]{:S(2)}) collective-permute-start(bf16[128,512]{0,1:T(8,128)(2,1)S(1)} %collective-permute-done.7), channel_id=1, source_target_pairs={{0,15},{1,0},{2,1},{3,2},{4,3},{5,4},{6,5},{7,6},{8,7},{9,8},{10,9... | collective-permute-start | bytes 393224 | tf_op jit(solution)/shard_map/ppermute | solution.py:23
  69.2 2.6 collective-permute-done.8
  71.8 0.0 collective-permute-start.10
  71.8 0.0 collective-permute-done.9
  71.8 5.6 %collective-permute-start.11 = (bf16[128,512]{0,1:T(8,128)(2,1)S(1)}, bf16[128,512]{0,1:T(8,128)(2,1)S(1)}, u32[]{:S(2)}, u32[]{:S(2)}) collective-permute-start(bf16[128,512]{0,1:T(8,128)(2,1)S(1)} %collective-permute-done.9), channel_id=1, source_target_pairs={{0,15},{1,0},{2,1},{3,2},{4,3},{5,4},{6,5},{7,6},{8,7},{9,8},{10,9... | collective-permute-start | bytes 393224 | tf_op jit(solution)/shard_map/ppermute | solution.py:23
  77.5 2.6 collective-permute-done.10
  80.1 0.0 collective-permute-start.12
  80.1 0.0 collective-permute-done.11
  80.1 5.6 %collective-permute-start.13 = (bf16[128,512]{0,1:T(8,128)(2,1)S(1)}, bf16[128,512]{0,1:T(8,128)(2,1)S(1)}, u32[]{:S(2)}, u32[]{:S(2)}) collective-permute-start(bf16[128,512]{0,1:T(8,128)(2,1)S(1)} %collective-permute-done.11), channel_id=1, source_target_pairs={{0,15},{1,0},{2,1},{3,2},{4,3},{5,4},{6,5},{7,6},{8,7},{9,8},{10,9... | collective-permute-start | bytes 393224 | tf_op jit(solution)/shard_map/ppermute | solution.py:23
  85.7 2.6 collective-permute-done.12
  88.4 0.0 collective-permute-start.14
  88.4 0.0 collective-permute-done.13
  88.4 8.2 %collective-permute-done.14 = bf16[128,512]{0,1:T(8,128)(2,1)S(1)} collective-permute-done((bf16[128,512]{0,1:T(8,128)(2,1)S(1)}, bf16[128,512]{0,1:T(8,128)(2,1)S(1)}, u32[]{:S(2)}, u32[]{:S(2)}) %collective-permute-start.14) | collective-permute-done | bytes 131104 | tf_op jit(solution)/shard_map/ppermute | solution.py:20
  96.7 1.1 fusion
  97.8 3.5 fusion.2
  101.2 30.8 %all_to_all.16 = bf16[128,8,1024]{0,2,1:T(8,128)(2,1)S(1)} all-to-all(bf16[128,8,1024]{0,2,1:T(8,128)(2,1)S(1)} %bitcast.25), channel_id=1, replica_groups=mesh['pair'=2,'batch'=4,'vocab'=16] {'pair','batch'}, dimensions={1} | all-to-all | bytes 4194304 | tf_op jit(solution)/shard_map/all_to_all | solution.py:37
  132.1 2.6 copy.16
  134.7 1.8 copy.17
  136.5 14.4 %fusion.6 = f32[1024,4096]{1,0:T(8,128)} fusion(bf16[1024,1024]{1,0:T(8,128)(2,1)S(1)} %bitcast.28, bf16[1024,4096]{1,0:T(8,128)(2,1)} %param.5), kind=kOutput, calls=%fused_computation.37 | convolution fusion | flops 8589934592 | bytes 27262976 | tf_op jit(solution)/shard_map/dot_general | solution.py:43
  150.9 0.0 reduce-scatter.2.cloned.1.call-update
  151.0 165.4 %reduce-scatter.2.cloned.1.call-done = f32[128,4096]{1,0:T(8,128)} async-done(((f32[1024,4096]{1,0:T(8,128)}), f32[128,4096]{1,0:T(8,128)}) %reduce-scatter.2.cloned.1.call-update) | async-done | bytes 2097168 | tf_op jit(solution)/shard_map/reduce_scatter | solution.py:42
  316.3 0.0 copy-start
  316.3 2.0 slice_reduce_fusion
  318.3 0.3 copy-done
  318.5 0.5 exponential_reduce_fusion.1
  319.1 23.5 %all-gather.2 = f32[16,4,64]{2,1,0:T(4,128)S(1)} all-gather(f32[1,4,64]{2,1,0:T(4,128)S(1)} %maximum_bitcast_fusion), channel_id=2, replica_groups=mesh['pair'=2,'batch'=4,'vocab'=16] {'vocab'}, dimensions={0}, use_global_device_ids=true | all-gather | bytes 17408 | tf_op jit(solution)/shard_map/all_gather | solution.py:56
  342.7 1.6 slice_subtract_fusion
  (24 shorter events, 0.5 us)
Async XLA Ops:
  7.2 309.2 %reduce-scatter.2.cloned.1.call-start = ((), (), s32[]{:S(2)}) async-start(), calls=%async_computation.2 | async-start | bytes 18874368 | tf_op jit(solution)/shard_map/reduce_scatter | solution.py:42
  8.2 28.6 %collective-permute-start = (bf16[128,512]{0,1:T(8,128)(2,1)S(1)}, bf16[128,512]{0,1:T(8,128)(2,1)S(1)}, u32[]{:S(2)}, u32[]{:S(2)}) collective-permute-start(bf16[128,512]{0,1:T(8,128)(2,1)S(1)} %bitcast.29), channel_id=1, source_target_pairs={{0,1},{1,2},{2,3},{3,4},{4,5},{5,6},{6,7},{7,8},{8,9},{9,10},{10,1... | collective-permute-start | bytes 393224 | tf_op jit(solution)/shard_map/ppermute | solution.py:20
  10.3 27.9 %collective-permute-start.1 = (bf16[128,512]{0,1:T(8,128)(2,1)S(1)}, bf16[128,512]{0,1:T(8,128)(2,1)S(1)}, u32[]{:S(2)}, u32[]{:S(2)}) collective-permute-start(bf16[128,512]{0,1:T(8,128)(2,1)S(1)} %bitcast.30), channel_id=1, source_target_pairs={{0,15},{1,0},{2,1},{3,2},{4,3},{5,4},{6,5},{7,6},{8,7},{9,8},{10,9... | collective-permute-start | bytes 393224 | tf_op jit(solution)/shard_map/ppermute | solution.py:23
  36.9 9.5 %collective-permute-start.2 = (bf16[128,512]{0,1:T(8,128)(2,1)S(1)}, bf16[128,512]{0,1:T(8,128)(2,1)S(1)}, u32[]{:S(2)}, u32[]{:S(2)}) collective-permute-start(bf16[128,512]{0,1:T(8,128)(2,1)S(1)} %collective-permute-done), channel_id=1, source_target_pairs={{0,1},{1,2},{2,3},{3,4},{4,5},{5,6},{6,7},{7,8},{8,9},{9,10},{10,1... | collective-permute-start | bytes 393224 | tf_op jit(solution)/shard_map/ppermute | solution.py:20
  38.2 8.2 %collective-permute-start.3 = (bf16[128,512]{0,1:T(8,128)(2,1)S(1)}, bf16[128,512]{0,1:T(8,128)(2,1)S(1)}, u32[]{:S(2)}, u32[]{:S(2)}) collective-permute-start(bf16[128,512]{0,1:T(8,128)(2,1)S(1)} %collective-permute-done.1), channel_id=1, source_target_pairs={{0,15},{1,0},{2,1},{3,2},{4,3},{5,4},{6,5},{7,6},{8,7},{9,8},{10,9... | collective-permute-start | bytes 393224 | tf_op jit(solution)/shard_map/ppermute | solution.py:23
  46.4 8.8 %collective-permute-start.4 = (bf16[128,512]{0,1:T(8,128)(2,1)S(1)}, bf16[128,512]{0,1:T(8,128)(2,1)S(1)}, u32[]{:S(2)}, u32[]{:S(2)}) collective-permute-start(bf16[128,512]{0,1:T(8,128)(2,1)S(1)} %collective-permute-done.2), channel_id=1, source_target_pairs={{0,1},{1,2},{2,3},{3,4},{4,5},{5,6},{6,7},{7,8},{8,9},{9,10},{10,1... | collective-permute-start | bytes 393224 | tf_op jit(solution)/shard_map/ppermute | solution.py:20
  46.4 8.8 %collective-permute-start.5 = (bf16[128,512]{0,1:T(8,128)(2,1)S(1)}, bf16[128,512]{0,1:T(8,128)(2,1)S(1)}, u32[]{:S(2)}, u32[]{:S(2)}) collective-permute-start(bf16[128,512]{0,1:T(8,128)(2,1)S(1)} %collective-permute-done.3), channel_id=1, source_target_pairs={{0,15},{1,0},{2,1},{3,2},{4,3},{5,4},{6,5},{7,6},{8,7},{9,8},{10,9... | collective-permute-start | bytes 393224 | tf_op jit(solution)/shard_map/ppermute | solution.py:23
  55.2 8.3 %collective-permute-start.6 = (bf16[128,512]{0,1:T(8,128)(2,1)S(1)}, bf16[128,512]{0,1:T(8,128)(2,1)S(1)}, u32[]{:S(2)}, u32[]{:S(2)}) collective-permute-start(bf16[128,512]{0,1:T(8,128)(2,1)S(1)} %collective-permute-done.4), channel_id=1, source_target_pairs={{0,1},{1,2},{2,3},{3,4},{4,5},{5,6},{6,7},{7,8},{8,9},{9,10},{10,1... | collective-permute-start | bytes 393224 | tf_op jit(solution)/shard_map/ppermute | solution.py:20
  55.2 8.3 %collective-permute-start.7 = (bf16[128,512]{0,1:T(8,128)(2,1)S(1)}, bf16[128,512]{0,1:T(8,128)(2,1)S(1)}, u32[]{:S(2)}, u32[]{:S(2)}) collective-permute-start(bf16[128,512]{0,1:T(8,128)(2,1)S(1)} %collective-permute-done.5), channel_id=1, source_target_pairs={{0,15},{1,0},{2,1},{3,2},{4,3},{5,4},{6,5},{7,6},{8,7},{9,8},{10,9... | collective-permute-start | bytes 393224 | tf_op jit(solution)/shard_map/ppermute | solution.py:23
  63.5 8.3 %collective-permute-start.8 = (bf16[128,512]{0,1:T(8,128)(2,1)S(1)}, bf16[128,512]{0,1:T(8,128)(2,1)S(1)}, u32[]{:S(2)}, u32[]{:S(2)}) collective-permute-start(bf16[128,512]{0,1:T(8,128)(2,1)S(1)} %collective-permute-done.6), channel_id=1, source_target_pairs={{0,1},{1,2},{2,3},{3,4},{4,5},{5,6},{6,7},{7,8},{8,9},{9,10},{10,1... | collective-permute-start | bytes 393224 | tf_op jit(solution)/shard_map/ppermute | solution.py:20
  63.5 8.3 %collective-permute-start.9 = (bf16[128,512]{0,1:T(8,128)(2,1)S(1)}, bf16[128,512]{0,1:T(8,128)(2,1)S(1)}, u32[]{:S(2)}, u32[]{:S(2)}) collective-permute-start(bf16[128,512]{0,1:T(8,128)(2,1)S(1)} %collective-permute-done.7), channel_id=1, source_target_pairs={{0,15},{1,0},{2,1},{3,2},{4,3},{5,4},{6,5},{7,6},{8,7},{9,8},{10,9... | collective-permute-start | bytes 393224 | tf_op jit(solution)/shard_map/ppermute | solution.py:23
  71.8 8.3 %collective-permute-start.10 = (bf16[128,512]{0,1:T(8,128)(2,1)S(1)}, bf16[128,512]{0,1:T(8,128)(2,1)S(1)}, u32[]{:S(2)}, u32[]{:S(2)}) collective-permute-start(bf16[128,512]{0,1:T(8,128)(2,1)S(1)} %collective-permute-done.8), channel_id=1, source_target_pairs={{0,1},{1,2},{2,3},{3,4},{4,5},{5,6},{6,7},{7,8},{8,9},{9,10},{10,1... | collective-permute-start | bytes 393224 | tf_op jit(solution)/shard_map/ppermute | solution.py:20
  71.8 8.3 %collective-permute-start.11 = (bf16[128,512]{0,1:T(8,128)(2,1)S(1)}, bf16[128,512]{0,1:T(8,128)(2,1)S(1)}, u32[]{:S(2)}, u32[]{:S(2)}) collective-permute-start(bf16[128,512]{0,1:T(8,128)(2,1)S(1)} %collective-permute-done.9), channel_id=1, source_target_pairs={{0,15},{1,0},{2,1},{3,2},{4,3},{5,4},{6,5},{7,6},{8,7},{9,8},{10,9... | collective-permute-start | bytes 393224 | tf_op jit(solution)/shard_map/ppermute | solution.py:23
  80.1 8.3 %collective-permute-start.12 = (bf16[128,512]{0,1:T(8,128)(2,1)S(1)}, bf16[128,512]{0,1:T(8,128)(2,1)S(1)}, u32[]{:S(2)}, u32[]{:S(2)}) collective-permute-start(bf16[128,512]{0,1:T(8,128)(2,1)S(1)} %collective-permute-done.10), channel_id=1, source_target_pairs={{0,1},{1,2},{2,3},{3,4},{4,5},{5,6},{6,7},{7,8},{8,9},{9,10},{10,1... | collective-permute-start | bytes 393224 | tf_op jit(solution)/shard_map/ppermute | solution.py:20
  80.1 8.3 %collective-permute-start.13 = (bf16[128,512]{0,1:T(8,128)(2,1)S(1)}, bf16[128,512]{0,1:T(8,128)(2,1)S(1)}, u32[]{:S(2)}, u32[]{:S(2)}) collective-permute-start(bf16[128,512]{0,1:T(8,128)(2,1)S(1)} %collective-permute-done.11), channel_id=1, source_target_pairs={{0,15},{1,0},{2,1},{3,2},{4,3},{5,4},{6,5},{7,6},{8,7},{9,8},{10,9... | collective-permute-start | bytes 393224 | tf_op jit(solution)/shard_map/ppermute | solution.py:23
  88.4 8.3 %collective-permute-start.14 = (bf16[128,512]{0,1:T(8,128)(2,1)S(1)}, bf16[128,512]{0,1:T(8,128)(2,1)S(1)}, u32[]{:S(2)}, u32[]{:S(2)}) collective-permute-start(bf16[128,512]{0,1:T(8,128)(2,1)S(1)} %collective-permute-done.12), channel_id=1, source_target_pairs={{0,1},{1,2},{2,3},{3,4},{4,5},{5,6},{6,7},{7,8},{8,9},{9,10},{10,1... | collective-permute-start | bytes 393224 | tf_op jit(solution)/shard_map/ppermute | solution.py:20
  316.3 2.2 copy-start
Sparse Core Ops, SparseCore 0:
  151.1 165.2 reduce-scatter.1
